TPU v7x, 32 devices: a whole 2x2x4 slice. The times are simulated.
32 devices in a mesh: rt: 8 (over y, x, core), ct: 4 (over z).
Axes of the slice: x: 2, y: 2, z: 4, core: 2. Of those that a mesh axis runs over, the one named last changes fastest.
Arguments:
- factor_rows: float32 [48, 2, 1024, 1024], P('rt', None, 'ct'), as said below
- slot_row: int32 [48], replicated, may hold values from -1 to 31, as said below
- known: float32 [48, 1024, 256], P('rt', 'ct'), may hold values from -6 to 6
- rhs: float32 [2, 1024, 256], P(None, 'ct', 'rt'), may hold values from -6 to 6
Outputs:
- solved: float32 [2, 1024, 256], P(None, 'ct', 'rt')
Inputs may be any that keep to these rules, and one draw needn't show every extreme that they name: `slot_row`: each row tile 0 to 31 stands in exactly one slot; the other slots hold -1. The slots of one index of rt are the 6 consecutive ones; at most 6 are live, and some index of rt has all 6 live. `factor_rows`: diagonal tiles L[0, 0] and L[1, 1] are lower triangular with diagonal entries from 1 to 2; the entry block (0, 1) is zero; entries of empty slots are arbitrary.
All inputs are finite; a program needn't handle non-finite values.
Results may differ from a plain program's by a relative error of at most 0.0003.
Values sent between devices are 32-bit elements; how exact they have to be, the bound alone decides.
No kernel may reach another device: no remote copies, remote signals or barrier semaphores. Data moves between devices by JAX's collectives and lax.ppermute only.
A program may use at most 64 MiB of HBM per device.

v0:
```python
import jax
import jax.numpy as jnp
from jax import lax
from jax.sharding import PartitionSpec as P


def spread(value, axis, root):
    mine = lax.axis_index(axis) == root
    return lax.psum(jnp.where(mine, value, jnp.zeros_like(value)), axis)


def shards(factor_rows, slot_row, known, rhs):
    high = lax.Precision.HIGHEST
    band = known.shape[1]
    columns = rhs.shape[2]
    slot_count = factor_rows.shape[0]
    offset = lax.axis_index("ct") * band
    col_offset = lax.axis_index("rt") * columns
    local_rows = lax.dynamic_slice_in_dim(
        slot_row, lax.axis_index("rt") * slot_count, slot_count, 0
    )
    live = (local_rows >= 2).astype(jnp.float32)
    masked = known * live[:, None, None]
    partial_value = jnp.einsum("scka,skr->car", factor_rows, masked, precision=high)
    pick_zero = local_rows == 0
    pick_one = local_rows == 1
    diag_zero = jnp.sum(jnp.where(pick_zero[:, None, None], factor_rows[:, 0], 0.0), 0)
    diag_one = jnp.sum(jnp.where(pick_one[:, None, None], factor_rows[:, 1], 0.0), 0)
    lower_one = jnp.sum(jnp.where(pick_one[:, None, None], factor_rows[:, 0], 0.0), 0)
    owner_zero = jnp.argmax(slot_row == 0) // slot_count
    owner_one = jnp.argmax(slot_row == 1) // slot_count
    tile_zero = spread(diag_zero, "rt", owner_zero)
    tile_one, tile_lower = (spread(diag_one, "rt", owner_one), spread(lower_one, "rt", owner_one))
    total = lax.psum(partial_value, ("rt", "ct"))
    rows_mine = lax.dynamic_slice_in_dim(total, offset, band, 1)
    mine = lax.dynamic_slice_in_dim(rows_mine, col_offset, columns, 2)
    residual = lax.all_gather(rhs - mine, "ct", axis=1, tiled=True)
    whole_zero, whole_one = (
        lax.all_gather(tile_zero, "ct", axis=0, tiled=True),
        lax.all_gather(tile_one, "ct", axis=0, tiled=True),
    )
    solved_one = lax.linalg.triangular_solve(
        whole_one, residual[1], left_side=True, lower=True, transpose_a=True
    )
    one_band = lax.dynamic_slice_in_dim(solved_one, offset, band, 0)
    coupling = jnp.einsum("ka,kr->ar", tile_lower, one_band, precision=high)
    coupled = lax.psum(coupling, "ct")
    solved_zero = lax.linalg.triangular_solve(
        whole_zero, residual[0] - coupled, left_side=True, lower=True, transpose_a=True
    )
    zero_band = lax.dynamic_slice_in_dim(solved_zero, offset, band, 0)
    return jnp.stack([zero_band, one_band])


def solution(mesh):
    in_specs = (P("rt", None, "ct", None), P(), P("rt", "ct", None), P(None, "ct", "rt"))
    out_specs = P(None, "ct", "rt")
    return jax.shard_map(shards, mesh=mesh, in_specs=in_specs, out_specs=out_specs, check_vma=False)
```

profile of v0, /device:TPU:0, one launch (start us, length us, event | category | flops | bytes accessed | tf_op | source)
XLA Modules:
  0.0 562.1 jit_solution(5160775739267857526)
XLA Ops:
  6.5 1.4 compare_reduce_fusion
  10.0 1.4 compare_reduce_fusion.1
  14.2 6.1 %fusion.2 = (f32[256,1024]{1,0:T(8,128)S(1)}, f32[256,1024]{1,0:T(8,128)S(1)}, f32[256,1024]{1,0:T(8,128)S(1)}) fusion(f32[6,2,256,1024]{3,2,1,0:T(8,128)} %param.6, pred[6]{0:T(512)(128)(4,1)S(1)} %get-tuple-element.53, pred[6]{0:T(512)(128)(4,1)S(1)} %get-tuple-element.54), kind=kLoop, calls=%fused_computation.9 | loop fusion | flops 8650752 | bytes 15728652 | tf_op jit(solution)/shard_map/reduce_sum | solution.py:29
  20.3 1.1 broadcast_select_fusion.2
  21.4 1.6 broadcast_select_fusion
  23.3 14.9 %convolution_bitcast_fusion = f32[2,1024,256]{1,2,0:T(8,128)} fusion(f32[6,2,256,1024]{3,2,1,0:T(8,128)} %param.6, f32[6,256,256]{2,1,0:T(8,128)S(1)} %copy-done, f32[6]{0:T(128)S(1)} %get-tuple-element.52), kind=kOutput, calls=%fused_computation.13 | convolution fusion | flops 9664069632 | bytes 16252952 | tf_op jit(solution)/shard_map/scka,skr->car/dot_general | solution.py:24
  38.3 57.5 %all-reduce.9.cloned.1.call-done = (f32[256,1024]{1,0:T(8,128)}, f32[256,1024]{1,0:T(8,128)}, f32[256,1024]{1,0:T(8,128)}) async-done(((f32[256,1024]{1,0:T(8,128)}, f32[256,1024]{1,0:T(8,128)}, f32[256,1024]{1,0:T(8,128)}), (f32[256,1024]{1,0:T(8,128)}, f32[256,1024]{1,0:T(8,128)}, f32[256,1024]{1,0:T(8,128)})) %all-reduce.9.cloned.1.call-update) | async-done | bytes 3145744 | tf_op jit(solution)/shard_map/psum | solution.py:9
  95.9 140.0 %all-reduce.5.cloned.1.call-done = f32[2,1024,256]{1,2,0:T(8,128)} async-done(((f32[2,1024,256]{1,2,0:T(8,128)}), f32[2,1024,256]{1,2,0:T(8,128)}) %all-reduce.5.cloned.1.call-update) | async-done | bytes 2097168 | tf_op jit(solution)/shard_map/psum | solution.py:34
  235.9 1.0 dynamic-slice_subtract_fusion
  236.9 14.7 %all_gather.10 = f32[2,1024,32]{1,2,0:T(8,128)S(1)} all-gather(f32[2,256,32]{1,2,0:T(8,128)S(1)} %dynamic-slice_subtract_fusion), channel_id=1, replica_groups=mesh['rt'=8,'ct'=4] {'ct'}, dimensions={1}, use_global_device_ids=true | all-gather | bytes 327680 | tf_op jit(solution)/shard_map/all_gather | solution.py:37
  251.8 66.0 %all-gather.5.cloned.1.call-done = f32[1024,1024]{1,0:T(8,128)} async-done(((f32[256,1024]{1,0:T(8,128)}), f32[1024,1024]{1,0:T(8,128)}) %all-gather.5.cloned.1.call-update) | async-done | bytes 4194320 | tf_op jit(solution)/shard_map/all_gather | solution.py:40
  317.8 4.7 fusion.3
  322.6 22.5 %while.4 = (s32[]{:T(128)}, f32[1024,1024]{1,0:T(8,128)}, s32[8,2]{0,1:T(2,128)S(1)}, f32[8,128,128]{2,1,0:T(8,128)S(1)}, s32[]{:T(128)}) while((s32[]{:T(128)}, f32[1024,1024]{1,0:T(8,128)}, s32[8,2]{0,1:T(2,128)S(1)}, f32[8,128,128]{2,1,0:T(8,128)S(1)}, s32[]{:T(128)}) %tuple.49), condition=%wide.while_cond, body=%wide.while_body.sunk | while | flops 2 | bytes 131181 | solution.py:42
  323.2 2.2 bitcast_dynamic-update-slice_fusion.4
  326.1 2.2 bitcast_dynamic-update-slice_fusion.4
  328.9 2.2 bitcast_dynamic-update-slice_fusion.4
  331.7 2.2 bitcast_dynamic-update-slice_fusion.4
  334.5 2.2 bitcast_dynamic-update-slice_fusion.4
  337.3 2.2 bitcast_dynamic-update-slice_fusion.4
  340.2 2.2 bitcast_dynamic-update-slice_fusion.4
  343.0 2.1 bitcast_dynamic-update-slice_fusion.4
  345.1 78.6 %custom-call.4 = f32[8,128,128]{1,2,0:T(8,128)S(1)} custom-call(f32[8,128,128]{2,1,0:T(8,128)S(1)} %get-tuple-element.24), custom_call_target="InvertDiagBlocksLowerTriangular" | custom-call | tf_op jit(solution)/shard_map/triangular_solve/custom-call.1 | solution.py:42
  423.9 1.0 convolution_subtract_fusion.7
  425.2 1.1 convolution_subtract_fusion.6
  426.5 1.2 convolution_subtract_fusion.5
  427.9 1.2 convolution_subtract_fusion.4
  429.4 1.3 convolution_subtract_fusion.13
  431.0 1.3 convolution_subtract_fusion.12
  432.6 1.4 convolution_subtract_fusion.11
  434.3 1.4 fusion.67
  435.8 4.7 fusion.4
  440.5 24.2 %while.5 = (s32[]{:T(128)}, f32[1024,1024]{1,0:T(8,128)}, s32[8,2]{0,1:T(2,128)S(1)}, f32[8,128,128]{2,1,0:T(8,128)S(1)}, s32[]{:T(128)}) while((s32[]{:T(128)}, f32[1024,1024]{1,0:T(8,128)}, s32[8,2]{0,1:T(2,128)S(1)}, f32[8,128,128]{2,1,0:T(8,128)S(1)}, s32[]{:T(128)}) %tuple.66), condition=%wide.while_cond.clone, body=%wide.while_body.clone.sunk | while | flops 2 | bytes 131181 | solution.py:48
  441.2 2.3 bitcast_dynamic-update-slice_fusion.5
  444.2 2.3 bitcast_dynamic-update-slice_fusion.5
  447.3 2.3 bitcast_dynamic-update-slice_fusion.5
  450.3 2.3 bitcast_dynamic-update-slice_fusion.5
  453.3 2.3 bitcast_dynamic-update-slice_fusion.5
  456.4 2.3 bitcast_dynamic-update-slice_fusion.5
  459.4 2.3 bitcast_dynamic-update-slice_fusion.5
  462.4 2.3 bitcast_dynamic-update-slice_fusion.5
  464.7 78.6 %custom-call.5 = f32[8,128,128]{1,2,0:T(8,128)S(1)} custom-call(f32[8,128,128]{2,1,0:T(8,128)S(1)} %get-tuple-element.25), custom_call_target="InvertDiagBlocksLowerTriangular" | custom-call | tf_op jit(solution)/shard_map/triangular_solve/custom-call.1 | solution.py:48
  544.5 1.0 convolution_subtract_fusion.3
  545.7 1.1 convolution_subtract_fusion.2
  547.0 1.2 convolution_subtract_fusion.1
  548.4 1.2 convolution_subtract_fusion
  550.0 1.3 convolution_subtract_fusion.10
  551.5 1.3 convolution_subtract_fusion.9
  553.2 1.4 convolution_subtract_fusion.8
  (120 shorter events, 16.7 us)
Async XLA Ops:
  6.5 89.3 %all-reduce.9.cloned.1.call-start = ((), (), s32[]{:S(2)}) async-start(), calls=%async_computation.4 | async-start | bytes 6291456 | tf_op jit(solution)/shard_map/psum | solution.py:9
  21.4 1.9 copy-start
  23.1 212.8 %all-reduce.5.cloned.1.call-start = ((), (), s32[]{:S(2)}) async-start(), calls=%async_computation.1 | async-start | bytes 4194304 | tf_op jit(solution)/shard_map/psum | solution.py:34
  23.3 212.6 %copy-start.2 = (f32[2,256,32]{1,2,0:T(8,128)S(1)}, f32[2,256,32]{1,2,0:T(8,128)}, u32[]{:S(2)}) copy-start(f32[2,256,32]{1,2,0:T(8,128)} %param.9) | copy-start | bytes 196612
  38.2 279.6 %all-gather.5.cloned.1.call-start = ((), (), s32[]{:S(2)}) async-start(), calls=%async_computation.2 | async-start | bytes 5242880 | tf_op jit(solution)/shard_map/all_gather | solution.py:40
  95.8 339.9 %all-gather.3.cloned.1.call-start = ((), (), s32[]{:S(2)}) async-start(), calls=%async_computation | async-start | bytes 5242880 | tf_op jit(solution)/shard_map/all_gather | solution.py:39
  251.6 291.7 %all-reduce.7.cloned.1.call-start = ((), (), s32[]{:S(2)}) async-start(), calls=%async_computation.3 | async-start | bytes 262144 | tf_op jit(solution)/shard_map/psum | solution.py:47
  322.6 111.8 %copy-start.1 = (f32[256,1024]{1,0:T(8,128)S(1)}, f32[256,1024]{1,0:T(8,128)}, u32[]{:S(2)}) copy-start(f32[256,1024]{1,0:T(8,128)} %get-tuple-element.47) | copy-start | bytes 3145732
Sparse Core Ops, SparseCore 0:
  23.2 72.5 all-reduce.8
  102.0 133.8 all-reduce.4
  237.5 80.3 all-gather.4
  319.2 79.3 all-gather.2
  435.9 33.0 all-reduce.6
where the time goes:
time: 564 us; the launch traced here: 562 us
  waiting for transfers between devices  264 us (47%)
  other arithmetic  182 us (32%)
  local copies, waits for them, and re-layouts  47 us (8%)
  matrix products  36.6 us (6%)
  between operations  18 us (3%)
  blocking collectives  14.7 us (3%)
    psum x1, waiting for transfers between devices, shards(): total = lax.psum(partial_value, ('rt', 'ct'))  140 us
    another operation x3, other arithmetic, shards(): lax.linalg.triangular_solve(whole_zero, residual[0] - coupled, left_side=...  83.3 us
    another operation x2, other arithmetic, shards(): lax.linalg.triangular_solve(whole_one, residual[1], left_side=True, lower...  83.3 us
    all_gather x1, waiting for transfers between devices, shards(): lax.all_gather(tile_one, 'ct', axis=0, tiled=True)  66 us
    psum x1, waiting for transfers between devices, spread(): return lax.psum(jnp.where(mine, value, jnp.zeros_like(value)), axis)  57.5 us
    another operation x31, local copies, waits for them, and re-layouts, shards(): lax.linalg.triangular_solve(whole_zero, residual[0] - coupled, left_side=...  24.1 us
    another operation x28, local copies, waits for them, and re-layouts, shards(): lax.linalg.triangular_solve(whole_one, residual[1], left_side=True, lower...  22.4 us
    dot_general x1, matrix products, shards(): jnp.einsum('scka,skr->car', factor_rows, masked, precision=high)  14.9 us
  transfers between devices with their start and end apart: 5, of which 3 were waited for; matrix products, arithmetic and copies ran while one was open for 43% of the time, Pallas kernels for 0%

commit v1 on v0

--- a/solution.py
+++ b/solution.py
@@ -31,7 +31,7 @@
     owner_one = jnp.argmax(slot_row == 1) // slot_count
     tile_zero = spread(diag_zero, "rt", owner_zero)
     tile_one, tile_lower = (spread(diag_one, "rt", owner_one), spread(lower_one, "rt", owner_one))
-    total = lax.psum(partial_value, ("rt", "ct"))
+    total = lax.psum(lax.psum(partial_value, "ct"), "rt")
     rows_mine = lax.dynamic_slice_in_dim(total, offset, band, 1)
     mine = lax.dynamic_slice_in_dim(rows_mine, col_offset, columns, 2)
     residual = lax.all_gather(rhs - mine, "ct", axis=1, tiled=True)

time: 564 us -> 537 us (0.952)
  waiting for transfers between devices: 264 us -> 238 us
    psum x1, waiting for transfers between devices: 140 us -> 75 us  [shards(): total = lax.psum(lax.psum(partial_value, 'ct'), 'rt')]
    psum x1, waiting for transfers between devices: 57.5 us -> 96.2 us  [spread(): return lax.psum(jnp.where(mine, value, jnp.zeros_like(value)), axis)]
  transfers between devices with their start and end apart: 5 -> 5, of which waited for: 3 -> 3; matrix products, arithmetic and copies ran while one was open for 43% -> 44% of each run, Pallas kernels for 0% -> 0%
where the time goes in v1:
time: 537 us; the launch traced here: 536 us
  waiting for transfers between devices  238 us (44%)
  other arithmetic  181 us (34%)
  local copies, waits for them, and re-layouts  46.8 us (9%)
  matrix products  37 us (7%)
  between operations  17.6 us (3%)
  blocking collectives  14.7 us (3%)
    psum x1, waiting for transfers between devices, spread(): return lax.psum(jnp.where(mine, value, jnp.zeros_like(value)), axis)  96.2 us
    another operation x3, other arithmetic, shards(): lax.linalg.triangular_solve(whole_zero, residual[0] - coupled, left_side=...  83.3 us
    another operation x2, other arithmetic, shards(): lax.linalg.triangular_solve(whole_one, residual[1], left_side=True, lower...  83.3 us
    psum x1, waiting for transfers between devices, shards(): total = lax.psum(lax.psum(partial_value, 'ct'), 'rt')  75 us
    all_gather x1, waiting for transfers between devices, shards(): lax.all_gather(tile_one, 'ct', axis=0, tiled=True)  67.1 us
    another operation x31, local copies, waits for them, and re-layouts, shards(): lax.linalg.triangular_solve(whole_zero, residual[0] - coupled, left_side=...  24.1 us
    another operation x28, local copies, waits for them, and re-layouts, shards(): lax.linalg.triangular_solve(whole_one, residual[1], left_side=True, lower...  22.4 us
    dot_general x1, matrix products, shards(): jnp.einsum('scka,skr->car', factor_rows, masked, precision=high)  15.3 us
  transfers between devices with their start and end apart: 5, of which 3 were waited for; matrix products, arithmetic and copies ran while one was open for 44% of the time, Pallas kernels for 0%

profile of v1, /device:TPU:0, one launch (start us, length us, event | category | flops | bytes accessed | tf_op | source)
XLA Modules:
  0.0 535.6 jit_solution(10742743628016142090)
XLA Ops:
  6.5 0.7 compare_convert_fusion
  7.3 15.3 %convolution_bitcast_fusion = f32[2,1024,256]{1,2,0:T(8,128)} fusion(f32[6,2,256,1024]{3,2,1,0:T(8,128)} %param.6, f32[6,256,256]{2,1,0:T(8,128)} %param.8, f32[6]{0:T(128)S(1)} %get-tuple-element.53), kind=kOutput, calls=%fused_computation.13 | convolution fusion | flops 9664069632 | bytes 16252952 | tf_op jit(solution)/shard_map/scka,skr->car/dot_general | solution.py:24
  27.7 6.5 %fusion.2 = (f32[256,1024]{1,0:T(8,128)S(1)}, f32[256,1024]{1,0:T(8,128)S(1)}, f32[256,1024]{1,0:T(8,128)S(1)}) fusion(f32[6,2,256,1024]{3,2,1,0:T(8,128)} %param.6, pred[6]{0:T(512)(128)(4,1)S(1)} %get-tuple-element.54, pred[6]{0:T(512)(128)(4,1)S(1)} %get-tuple-element.55), kind=kLoop, calls=%fused_computation.9 | loop fusion | flops 8650752 | bytes 15728652 | tf_op jit(solution)/shard_map/reduce_sum | solution.py:29
  34.2 1.1 broadcast_select_fusion.2
  35.3 1.6 broadcast_select_fusion
  37.0 75.0 %all-reduce.5.cloned.1.call-done = f32[2,1024,256]{1,2,0:T(8,128)} async-done(((f32[2,1024,256]{1,2,0:T(8,128)}), f32[2,1024,256]{1,2,0:T(8,128)}) %all-reduce.5.cloned.1.call-update) | async-done | bytes 2097168 | tf_op jit(solution)/shard_map/psum | solution.py:34
  112.0 96.2 %all-reduce.9.cloned.1.call-done = (f32[256,1024]{1,0:T(8,128)}, f32[2,1024,256]{1,2,0:T(8,128)}, f32[256,1024]{1,0:T(8,128)}, f32[256,1024]{1,0:T(8,128)}) async-done(((f32[256,1024]{1,0:T(8,128)}, f32[2,1024,256]{1,2,0:T(8,128)}, f32[256,1024]{1,0:T(8,128)}, f32[256,1024]{1,0:T(8,128)}), (f32[256,1024]{1,0:T(8,128)}, f32[2,1024,256]{1,2,0:T(8,128)}, f32[256,1024]{1,0:T(8,128)}, ...) | async-done | bytes 5242896 | tf_op jit(solution)/shard_map/psum | solution.py:9
  208.4 1.0 dynamic-slice_subtract_fusion
  209.4 14.7 %all_gather.10 = f32[2,1024,32]{1,2,0:T(8,128)S(1)} all-gather(f32[2,256,32]{1,2,0:T(8,128)S(1)} %dynamic-slice_subtract_fusion), channel_id=1, replica_groups=mesh['rt'=8,'ct'=4] {'ct'}, dimensions={1}, use_global_device_ids=true | all-gather | bytes 327680 | tf_op jit(solution)/shard_map/all_gather | solution.py:37
  224.3 67.1 %all-gather.5.cloned.1.call-done = f32[1024,1024]{1,0:T(8,128)} async-done(((f32[256,1024]{1,0:T(8,128)}), f32[1024,1024]{1,0:T(8,128)}) %all-gather.5.cloned.1.call-update) | async-done | bytes 4194320 | tf_op jit(solution)/shard_map/all_gather | solution.py:40
  291.4 4.7 fusion.3
  296.2 22.5 %while.4 = (s32[]{:T(128)}, f32[1024,1024]{1,0:T(8,128)}, s32[8,2]{0,1:T(2,128)S(1)}, f32[8,128,128]{2,1,0:T(8,128)S(1)}, s32[]{:T(128)}) while((s32[]{:T(128)}, f32[1024,1024]{1,0:T(8,128)}, s32[8,2]{0,1:T(2,128)S(1)}, f32[8,128,128]{2,1,0:T(8,128)S(1)}, s32[]{:T(128)}) %tuple.49), condition=%wide.while_cond, body=%wide.while_body.sunk | while | flops 2 | bytes 131181 | solution.py:42
  296.8 2.2 bitcast_dynamic-update-slice_fusion.4
  299.6 2.2 bitcast_dynamic-update-slice_fusion.4
  302.5 2.2 bitcast_dynamic-update-slice_fusion.4
  305.3 2.2 bitcast_dynamic-update-slice_fusion.4
  308.1 2.2 bitcast_dynamic-update-slice_fusion.4
  310.9 2.2 bitcast_dynamic-update-slice_fusion.4
  313.7 2.2 bitcast_dynamic-update-slice_fusion.4
  316.6 2.1 bitcast_dynamic-update-slice_fusion.4
  318.7 78.6 %custom-call.4 = f32[8,128,128]{1,2,0:T(8,128)S(1)} custom-call(f32[8,128,128]{2,1,0:T(8,128)S(1)} %get-tuple-element.24), custom_call_target="InvertDiagBlocksLowerTriangular" | custom-call | tf_op jit(solution)/shard_map/triangular_solve/custom-call.1 | solution.py:42
  397.5 1.0 convolution_subtract_fusion.7
  398.7 1.1 convolution_subtract_fusion.6
  400.1 1.2 convolution_subtract_fusion.5
  401.5 1.2 convolution_subtract_fusion.4
  403.0 1.3 convolution_subtract_fusion.13
  404.6 1.3 convolution_subtract_fusion.12
  406.2 1.4 convolution_subtract_fusion.11
  407.9 1.4 fusion.67
  409.3 4.7 fusion.4
  414.1 24.2 %while.5 = (s32[]{:T(128)}, f32[1024,1024]{1,0:T(8,128)}, s32[8,2]{0,1:T(2,128)S(1)}, f32[8,128,128]{2,1,0:T(8,128)S(1)}, s32[]{:T(128)}) while((s32[]{:T(128)}, f32[1024,1024]{1,0:T(8,128)}, s32[8,2]{0,1:T(2,128)S(1)}, f32[8,128,128]{2,1,0:T(8,128)S(1)}, s32[]{:T(128)}) %tuple.66), condition=%wide.while_cond.clone, body=%wide.while_body.clone.sunk | while | flops 2 | bytes 131181 | solution.py:48
  414.8 2.3 bitcast_dynamic-update-slice_fusion.5
  417.8 2.3 bitcast_dynamic-update-slice_fusion.5
  420.9 2.3 bitcast_dynamic-update-slice_fusion.5
  423.9 2.3 bitcast_dynamic-update-slice_fusion.5
  426.9 2.3 bitcast_dynamic-update-slice_fusion.5
  429.9 2.3 bitcast_dynamic-update-slice_fusion.5
  433.0 2.3 bitcast_dynamic-update-slice_fusion.5
  436.0 2.3 bitcast_dynamic-update-slice_fusion.5
  438.3 78.6 %custom-call.5 = f32[8,128,128]{1,2,0:T(8,128)S(1)} custom-call(f32[8,128,128]{2,1,0:T(8,128)S(1)} %get-tuple-element.25), custom_call_target="InvertDiagBlocksLowerTriangular" | custom-call | tf_op jit(solution)/shard_map/triangular_solve/custom-call.1 | solution.py:48
  516.9 0.9 fusion.20
  518.1 1.0 convolution_subtract_fusion.3
  519.3 1.1 convolution_subtract_fusion.2
  520.6 1.2 convolution_subtract_fusion.1
  522.0 1.2 convolution_subtract_fusion
  523.5 1.3 convolution_subtract_fusion.10
  525.1 1.3 convolution_subtract_fusion.9
  526.7 1.4 convolution_subtract_fusion.8
  (120 shorter events, 16.2 us)
Async XLA Ops:
  6.5 105.4 %all-reduce.5.cloned.1.call-start = ((), (), s32[]{:S(2)}) async-start(), calls=%async_computation.1 | async-start | bytes 4194304 | tf_op jit(solution)/shard_map/psum | solution.py:34
  7.3 15.4 %copy-start.2 = (s32[48]{0:T(128)S(1)}, s32[48]{0:T(128)}, u32[]{:S(2)}) copy-start(s32[48]{0:T(128)} %param.7) | copy-start | bytes 580
  22.6 185.7 %all-reduce.9.cloned.1.call-start = ((), (), s32[]{:S(2)}) async-start(), calls=%async_computation.4 | async-start | bytes 10485760 | tf_op jit(solution)/shard_map/psum | solution.py:9
  37.0 171.4 %copy-start.1 = (f32[2,256,32]{1,2,0:T(8,128)S(1)}, f32[2,256,32]{1,2,0:T(8,128)}, u32[]{:S(2)}) copy-start(f32[2,256,32]{1,2,0:T(8,128)} %param.9) | copy-start | bytes 196612
  112.0 179.4 %all-gather.5.cloned.1.call-start = ((), (), s32[]{:S(2)}) async-start(), calls=%async_computation.2 | async-start | bytes 5242880 | tf_op jit(solution)/shard_map/all_gather | solution.py:40
  208.3 201.1 %all-gather.3.cloned.1.call-start = ((), (), s32[]{:S(2)}) async-start(), calls=%async_computation | async-start | bytes 5242880 | tf_op jit(solution)/shard_map/all_gather | solution.py:39
  224.1 292.8 %all-reduce.7.cloned.1.call-start = ((), (), s32[]{:S(2)}) async-start(), calls=%async_computation.3 | async-start | bytes 262144 | tf_op jit(solution)/shard_map/psum | solution.py:47
  296.1 111.8 %copy-start = (f32[256,1024]{1,0:T(8,128)S(1)}, f32[256,1024]{1,0:T(8,128)}, u32[]{:S(2)}) copy-start(f32[256,1024]{1,0:T(8,128)} %get-tuple-element.48) | copy-start | bytes 3145732
Sparse Core Ops, SparseCore 0:
  22.7 89.1 all-reduce.4
  116.1 92.1 all-reduce.8
  209.8 81.5 all-gather.4
  292.8 78.8 all-gather.2
  409.4 32.4 all-reduce.6
